TPU v7x, 256 devices: a whole 4x4x8 slice. The times are simulated.
256 devices in a mesh: row: 32 (over y, x, core), col: 8 (over z).
Axes of the slice: x: 4, y: 4, z: 8, core: 2. Of those that a mesh axis runs over, the one named last changes fastest.
Arguments:
- hidden: bfloat16 [2048, 2560], P(None, 'row'), may hold values from -6 to 6
- w_qkv: bfloat16 [2560, 3584], P('row', 'col'), may hold values from -8 to 8
- page_table: int32 [64, 64], P('row'), may hold values from -1 to 127, as said below
- prompt_lengths: int32 [64], P('row'), may hold values from 1 to 8192, as said below
- page_keys: bfloat16 [32, 128, 128, 512], P('row', 'col'), may hold values from -4 to 4
- page_values: bfloat16 [32, 128, 128, 512], P('row', 'col'), may hold values from -6 to 6
- tail_lengths: int32 [64, 16], P('row'), may hold values from 0 to 512
- tail_keys: bfloat16 [64, 16, 512, 512], P('row', 'col'), may hold values from -6 to 6
- tail_values: bfloat16 [64, 16, 512, 512], P('row', 'col'), may hold values from -6 to 6
Outputs:
- attended: bfloat16 [64, 16, 2, 2560], P('row', 'col')
Inputs may be any that keep to these rules, and one draw needn't show every extreme that they name: `page_table`: entry j of prompt p is the slot of block p // 2 that holds its tokens j * 128 to (j + 1) * 128 - 1 where j * 128 < prompt_lengths[p], else -1; the live slots of a block are distinct. Slot k of a block lies on the device of col index k // 16. The live pages of a block fill the devices' slots one device after another, in an order drawn from the seed, so that at least one device holds 16 live pages. `prompt_lengths`: every block of 2 prompts holds a prompt of 8192 tokens.
All inputs are finite; a program needn't handle non-finite values.
Results may differ from a plain program's by a relative error of at most 0.015.
The roundings to bfloat16 on the way count: a program that leaves them out, or rounds other values in their place, can miss the bound.
Values may be sent and summed in bfloat16 or wider, within the bound.
A program may use at most 64 MiB of HBM per device.

v0:
```python
import math
import jax
import jax.numpy as jnp
from jax import lax
from jax.sharding import PartitionSpec as P

HEADS = 20
KVH = 4
HD = 128
SAMPLES = 16
rope_base = 500000.0
masked_score = -1e30


def merged(value, axis, join):
    pieces = jax.tree.map(lambda part: lax.all_gather(part, axis), value)
    head = jax.tree.map(lambda part: part[0], pieces)
    tail = jax.tree.map(lambda part: part[1:], pieces)
    total, _ = lax.scan(lambda total, section: (join(total, section), None), head, tail)
    return total


def rotate(vectors, positions):
    half_size = vectors.shape[-1] // 2
    frequency = jnp.exp(
        jnp.arange(half_size, dtype=jnp.float32) * (-2.0 * math.log(rope_base) / vectors.shape[-1])
    )
    angles = positions.astype(jnp.float32)[..., None, None] * frequency
    cosine = jnp.cos(angles)
    sines = jnp.sin(angles)
    leading = vectors[..., :half_size].astype(jnp.float32)
    trailing = vectors[..., half_size:].astype(jnp.float32)
    return jnp.concatenate(
        [leading * cosine - trailing * sines, trailing * cosine + leading * sines], axis=-1
    )


def combine_states(earlier, later):
    top_early, sums_early, acc_early = earlier
    top_late, sums_late, acc_late = later
    highest = jnp.maximum(top_early, top_late)
    scale_early = jnp.exp(top_early - highest)
    scale_late = jnp.exp(top_late - highest)
    return (
        highest,
        sums_early * scale_early + sums_late * scale_late,
        acc_early * scale_early[..., None] + acc_late * scale_late[..., None],
    )


def project_rows(hidden, weights):
    return jnp.dot(hidden, weights, preferred_element_type=jnp.float32)


def local(
    hidden,
    w_qkv,
    page_table,
    prompt_lengths,
    page_keys,
    page_values,
    tail_lengths,
    tail_keys,
    tail_values,
):
    group_size = HEADS // KVH
    q_width = HEADS * HD
    kv_width = KVH * HD
    score_scale = 1.0 / math.sqrt(HD)
    column_sums = lax.psum_scatter(
        project_rows(hidden, w_qkv), "row", scatter_dimension=0, tiled=True
    ).astype(jnp.bfloat16)
    projected = lax.all_gather(column_sums, "col", axis=1, tiled=True)
    prompts_here = prompt_lengths.shape[0]
    projected = projected.reshape(prompts_here, SAMPLES, 2, projected.shape[-1])
    steps_ahead = jnp.arange(2, dtype=jnp.int32)
    positions = (
        prompt_lengths[:, None, None] + tail_lengths[:, :, None] + steps_ahead[None, None, :]
    )
    queries = rotate(
        projected[..., :q_width].reshape(prompts_here, SAMPLES, 2, HEADS, HD), positions
    ).astype(jnp.bfloat16)
    new_keys = rotate(
        projected[..., q_width : q_width + kv_width].reshape(prompts_here, SAMPLES, 2, KVH, HD),
        positions,
    ).astype(jnp.bfloat16)
    new_values = projected[..., q_width + kv_width :].reshape(prompts_here, SAMPLES, 2, KVH, HD)
    pool_keys = page_keys[0]
    pool_values = page_values[0]
    pool_slots = pool_keys.shape[0]
    page_size = pool_keys.shape[1]
    slot_ids = lax.axis_index("col") * pool_slots + jnp.arange(pool_slots, dtype=jnp.int32)
    matches = (page_table[None, :, :] == slot_ids[:, None, None]).astype(jnp.int32)
    owners = jnp.sum(matches, axis=2)
    page_index = jnp.sum(
        matches * jnp.arange(page_table.shape[1], dtype=jnp.int32)[None, None, :], axis=(1, 2)
    )
    slot_prompt = jnp.sum(owners * jnp.arange(prompts_here, dtype=jnp.int32)[None, :], axis=1)
    slot_length = jnp.sum(owners * prompt_lengths[None, :], axis=1)
    key_positions = (
        page_index[:, None] * page_size + jnp.arange(page_size, dtype=jnp.int32)[None, :]
    )
    visible = (key_positions < slot_length[:, None])[:, None, None, None, :]
    query_grid = queries.reshape(prompts_here, SAMPLES * 2, KVH, group_size, HD)
    slot_queries = jnp.take(query_grid, slot_prompt, axis=0)
    page_scores = (
        jnp.einsum(
            "sqkgd,spkd->sqkgp",
            slot_queries,
            pool_keys.reshape(pool_slots, page_size, KVH, HD),
            preferred_element_type=jnp.float32,
        )
        * score_scale
    )
    page_scores = jnp.where(visible, page_scores, masked_score)
    slot_top = jnp.max(page_scores, axis=-1)
    prompt_top = jnp.max(
        jnp.where(owners[:, :, None, None, None] > 0, slot_top[:, None], masked_score), axis=0
    )
    slot_shift = jnp.take(prompt_top, slot_prompt, axis=0)
    page_weights = jnp.where(visible, jnp.exp(page_scores - slot_shift[..., None]), 0.0)
    slot_sums = jnp.sum(page_weights, axis=-1)
    slot_acc = jnp.einsum(
        "sqkgp,spkd->sqkgd",
        page_weights.astype(jnp.bfloat16),
        pool_values.reshape(pool_slots, page_size, KVH, HD),
        preferred_element_type=jnp.float32,
    )
    owner_float = owners.astype(jnp.float32)
    prefix_sums = jnp.einsum(
        "sr,sqkg->rqkg", owner_float, slot_sums, precision=lax.Precision.HIGHEST
    )
    prefix_acc = jnp.einsum(
        "sr,sqkgd->rqkgd", owner_float, slot_acc, precision=lax.Precision.HIGHEST
    )
    state_shape = (prompts_here, SAMPLES, 2, KVH, group_size)
    prefix_top = prompt_top.reshape(state_shape)
    prefix_sums = prefix_sums.reshape(state_shape)
    prefix_acc = prefix_acc.reshape(state_shape + (HD,))
    own_count = tail_keys.shape[1]
    own_start = lax.axis_index("col") * own_count
    whole_top, whole_sums, whole_acc = merged(
        (prefix_top, prefix_sums, prefix_acc), "col", combine_states
    )
    merged_top = lax.dynamic_slice_in_dim(whole_top, own_start, own_count, 1)
    merged_sums = lax.dynamic_slice_in_dim(whole_sums, own_start, own_count, 1)
    merged_acc = lax.dynamic_slice_in_dim(whole_acc, own_start, own_count, 1)
    own_queries = lax.dynamic_slice_in_dim(queries, own_start, own_count, 1).reshape(
        prompts_here, own_count, 2, KVH, group_size, HD
    )
    own_keys = lax.dynamic_slice_in_dim(new_keys, own_start, own_count, 1)
    own_values = lax.dynamic_slice_in_dim(new_values, own_start, own_count, 1)
    own_tails = lax.dynamic_slice_in_dim(tail_lengths, own_start, own_count, 1)
    tail_room = tail_keys.shape[2]
    tail_grid = tail_keys.reshape(prompts_here, own_count, tail_room, KVH, HD)
    tail_scores = (
        jnp.einsum(
            "rstkgd,rsjkd->rstkgj", own_queries, tail_grid, preferred_element_type=jnp.float32
        )
        * score_scale
    )
    tail_seen = (jnp.arange(tail_room, dtype=jnp.int32)[None, None, :] < own_tails[:, :, None])[
        :, :, None, None, None, :
    ]
    tail_scores = jnp.where(tail_seen, tail_scores, masked_score)
    fresh_scores = (
        jnp.einsum(
            "rstkgd,rsukd->rstkgu", own_queries, own_keys, preferred_element_type=jnp.float32
        )
        * score_scale
    )
    causal = (steps_ahead[None, :] <= steps_ahead[:, None])[None, None, :, None, None, :]
    fresh_scores = jnp.where(causal, fresh_scores, masked_score)
    local_top = jnp.maximum(jnp.max(tail_scores, axis=-1), jnp.max(fresh_scores, axis=-1))
    tail_weights = jnp.where(tail_seen, jnp.exp(tail_scores - local_top[..., None]), 0.0)
    fresh_weights = jnp.where(causal, jnp.exp(fresh_scores - local_top[..., None]), 0.0)
    local_sums = jnp.sum(tail_weights, axis=-1) + jnp.sum(fresh_weights, axis=-1)
    local_acc = jnp.einsum(
        "rstkgj,rsjkd->rstkgd",
        tail_weights.astype(jnp.bfloat16),
        tail_values.reshape(prompts_here, own_count, tail_room, KVH, HD),
        preferred_element_type=jnp.float32,
    )
    local_acc = local_acc + jnp.einsum(
        "rstkgu,rsukd->rstkgd",
        fresh_weights.astype(jnp.bfloat16),
        own_values,
        preferred_element_type=jnp.float32,
    )
    final_top, final_sums, final_acc = combine_states(
        (merged_top, merged_sums, merged_acc), (local_top, local_sums, local_acc)
    )
    attended = final_acc / final_sums[..., None]
    return attended.reshape(prompts_here, own_count, 2, HEADS * HD).astype(jnp.bfloat16)


def solution(mesh):
    in_specs = (
        P(None, "row"),
        P("row", "col"),
        P("row", None),
        P("row"),
        P("row", "col", None, None),
        P("row", "col", None, None),
        P("row", None),
        P("row", "col", None, None),
        P("row", "col", None, None),
    )
    out_specs = P("row", "col", None, None)
    return jax.shard_map(local, mesh=mesh, in_specs=in_specs, out_specs=out_specs, check_vma=False)
```

profile of v0, /device:TPU:6, one launch (start us, length us, event | category | flops | bytes accessed | tf_op | source)
XLA Modules:
  0.0 266.6 jit_solution(7269477015864981519)
XLA Ops:
  6.5 1.0 copy-done
  7.5 3.6 %fusion.110 = f32[2048,448]{1,0:T(8,128)} fusion(bf16[2048,80]{0,1:T(8,128)(2,1)S(1)} %copy-done, bf16[80,448]{1,0:T(8,128)(2,1)} %param.12), kind=kOutput, calls=%fused_computation.142 | convolution fusion | flops 146800640 | bytes 4069376 | tf_op jit(solution)/shard_map/dot_general | solution.py:52
  11.2 2.1 reshape_squeeze.6
  13.3 4.0 %reshape_squeeze.7 = bf16[16,128,4,128]{3,2,1,0:T(4,128)(2,1)} reshape(bf16[1,16,128,512]{3,2,1,0:T(8,128)(2,1)} %param.16) | data formatting | bytes 4194304 | tf_op jit(solution)/shard_map/reshape;squeeze | solution.py:126
  17.3 0.2 fusion.80
  17.8 0.2 multiply_cosine_fusion
  18.0 85.4 %reduce-scatter.2.cloned.1.call-done = f32[64,448]{1,0:T(8,128)} async-done(((f32[2048,448]{1,0:T(8,128)}), f32[64,448]{1,0:T(8,128)}) %reduce-scatter.2.cloned.1.call-update) | async-done | bytes 114704 | tf_op jit(solution)/shard_map/reduce_scatter | solution.py:70
  103.4 0.9 convert_bitcast_fusion
  104.4 26.7 %all-gather.1 = bf16[8,448,64]{1,2,0:T(8,128)(2,1)S(1)} all-gather(bf16[1,448,64]{1,2,0:T(8,128)(2,1)S(1)} %convert_bitcast_fusion), channel_id=1, replica_groups=mesh['row'=32,'col'=8] {'col'}, dimensions={0}, use_global_device_ids=true | all-gather | bytes 516096 | tf_op jit(solution)/shard_map/all_gather | solution.py:73
  131.1 0.3 copy.171
  131.4 0.6 reshape.176
  132.1 0.8 copy-done.6
  133.0 0.2 slice.58
  133.2 0.2 reshape.184
  133.6 0.3 fusion.63
  133.9 0.3 copy.174
  134.2 0.3 copy.173
  134.7 0.2 copy-done.3
  134.9 0.2 pad_maximum_fusion
  135.0 1.1 gather_fusion
  136.1 5.7 %bitcast_reduce_fusion = (f32[16,32,4,5]{1,3,2,0:T(8,128)S(1)}, f32[16,4,32,5,128]{4,2,3,1,0:T(8,128)}) fusion(pred[16,128]{1,0:T(8,128)(4,1)S(1)} %add_compare_fusion, bf16[16,128,4,128,1]{3,2,1,0,4:T(4,128)(2,1)} %bitcast.114, bf16[16,32,4,5,128]{4,1,3,2,0:T(8,128)(2,1)S(1)} %gather_fusion, pred[16]{0:T(512)(128)(4,1)S(1)} %compare_and_fusion), kind=kOutput, calls=%fused_computation.13 | convolution fusion | flops 340776960 | bytes 10004496 | tf_op jit(solution)/shard_map/sqkgd,spkd->sqkgp/dot_general | solution.py:107
  142.0 0.6 gather_fusion.1
  142.8 4.2 %fusion.21 = f32[16,32,4,5,128]{4,1,3,2,0:T(8,128)S(1)} fusion(f32[16,4,32,5,128]{4,2,3,1,0:T(8,128)} %get-tuple-element.131, f32[16,32,4,5]{1,3,2,0:T(8,128)S(1)} %copy.180, pred[16,128]{1,0:T(8,128)(4,1)S(1)} %add_compare_fusion, bf16[16,128,4,128,1]{3,2,1,0,4:T(4,128)(2,1)} %bitcast.113), kind=kOutput, calls=%fused_computation.31 | convolution fusion | flops 342097920 | bytes 12625920 | tf_op jit(solution)/shard_map/sqkgp,spkd->sqkgd/dot_general | solution.py:123
  147.0 7.4 %fusion.6 = f32[2,32,4,5,128]{4,0,3,2,1:T(2,128)S(1)} fusion(f32[16,32,4,5,128]{4,1,3,2,0:T(8,128)S(1)} %fusion.21, s32[16,2]{0,1:T(2,128)S(1)} %get-tuple-element.90), kind=kOutput, calls=%fused_computation.16 | convolution fusion | flops 31457312 | bytes 5898368 | tf_op jit(solution)/shard_map/sr,sqkgd->rqkgd/dot_general | solution.py:133
  154.4 1.0 copy.186
  155.5 2.6 reshape.151
  158.0 4.0 %reshape.153 = bf16[2,2,512,4,128]{4,3,2,1,0:T(4,128)(2,1)} reshape(bf16[2,2,512,512]{3,2,1,0:T(8,128)(2,1)} %param.19) | data formatting | bytes 4194304 | tf_op jit(solution)/shard_map/reshape | solution.py:181
  162.2 0.8 copy.177
  163.0 5.9 %fusion.9 = f32[16,32,4,5]{1,3,2,0:T(8,128)} fusion(f32[16,4,32,5,128]{4,2,3,1,0:T(8,128)} %get-tuple-element.131, f32[16,32,4,5]{1,3,2,0:T(8,128)S(1)} %copy.180, pred[16,128]{1,0:T(8,128)(4,1)S(1)} %add_compare_fusion), kind=kLoop, calls=%fused_computation.20 | loop fusion | flops 6543360 | bytes 5326848 | tf_op jit(solution)/shard_map/reduce_sum | solution.py:122
  168.8 1.1 copy.181
  170.0 2.4 fusion.66
  172.4 26.0 %all-gather = f32[16,16,2,4,5]{1,3,4,2,0:T(4,128)S(1)} all-gather(f32[2,16,2,4,5]{1,3,4,2,0:T(4,128)S(1)} %copy.183), channel_id=2, replica_groups=mesh['row'=32,'col'=8] {'col'}, dimensions={0}, use_global_device_ids=true | all-gather | bytes 46080 | tf_op jit(solution)/shard_map/all_gather | solution.py:16
  198.4 1.6 fusion.105
  200.0 1.5 reshape.185
  201.6 1.1 copy.178
  202.7 26.0 %all_gather.13 = f32[8,2,16,2,4,5]{2,4,5,3,1,0:T(4,128)S(1)} all-gather(f32[1,2,16,2,4,5]{2,4,5,3,1,0:T(4,128)S(1)} %copy.178), channel_id=1, replica_groups=mesh['row'=32,'col'=8] {'col'}, dimensions={0}, use_global_device_ids=true | all-gather | bytes 46080 | tf_op jit(solution)/shard_map/all_gather | solution.py:16
  228.7 1.1 fusion.107
  229.8 0.8 fusion.73
  230.7 0.4 fusion.109
  231.1 0.8 fusion.108
  232.0 0.3 fusion.64
  232.3 1.0 convolution_bitcast_fusion
  233.3 1.1 slice_bitcast_fusion
  234.5 0.2 copy.187
  234.8 5.0 %slice.66 = f32[7,2,16,2,4,5,128]{6,2,5,4,3,1,0:T(8,128)} slice(f32[8,2,16,2,4,5,128]{6,2,5,4,3,1,0:T(8,128)} %all-gather.4.cloned.1.call-done), slice={[1:8], [0:2], [0:16], [0:2], [0:4], [0:5], [0:128]} | slice | bytes 9175040 | tf_op jit(solution)/shard_map/slice | solution.py:18
  239.8 16.7 %while.14 = (s32[]{:T(128)}, f32[2,16,2,4,5]{1,3,4,2,0:T(4,128)S(1)}, f32[2,16,2,4,5]{1,3,4,2,0:T(4,128)S(1)}, f32[2,16,2,4,5,128]{5,4,3,2,1,0:T(8,128)S(1)}, f3...) while((s32[]{:T(128)}, ...), condition=%wide.region_9.10_spmd, body=%wide.region_8.9_spmd.sunk | while | flops 499202 | bytes 3348581 | solution.py:19
  240.2 1.1 constant_dynamic-slice_fusion.3
  241.4 0.8 fusion.117
  242.6 1.1 constant_dynamic-slice_fusion.3
  243.8 0.8 fusion.117
  245.0 1.1 constant_dynamic-slice_fusion.3
  246.1 0.8 fusion.117
  247.4 1.1 constant_dynamic-slice_fusion.3
  248.5 0.8 fusion.117
  249.8 1.1 constant_dynamic-slice_fusion.3
  250.9 0.8 fusion.117
  252.2 1.1 constant_dynamic-slice_fusion.3
  253.3 0.8 fusion.117
  254.6 1.1 constant_dynamic-slice_fusion.3
  255.7 0.8 fusion.117
  256.5 0.2 copy.190
  256.7 0.2 copy.202
  256.9 2.1 fusion.55
  259.1 0.7 convert_element_type.59
  (83 shorter events, 4.9 us)
Async XLA Ops:
  6.5 1.0 copy-start
  6.5 4.6 %copy-start.5 = (bf16[1,16,128,512]{3,2,1,0:T(8,128)(2,1)S(1)}, bf16[1,16,128,512]{3,2,1,0:T(8,128)(2,1)}, u32[]{:S(2)}) copy-start(bf16[1,16,128,512]{3,2,1,0:T(8,128)(2,1)} %param.15) | copy-start | bytes 6291460
  6.5 96.9 %reduce-scatter.2.cloned.1.call-start = ((), (), s32[]{:S(2)}) async-start(), calls=%async_computation.1 | async-start | bytes 4325376 | tf_op jit(solution)/shard_map/reduce_scatter | solution.py:70
  11.1 222.2 %all-gather.4.cloned.1.call-start = ((), (), s32[]{:S(2)}) async-start(), calls=%async_computation.2 | async-start | bytes 5898240 | tf_op jit(solution)/shard_map/all_gather | solution.py:16
  11.2 6.1 %copy-start.12 = (s32[2,64]{1,0:T(2,128)S(1)}, s32[2,64]{1,0:T(2,128)}, u32[]{:S(2)}) copy-start(s32[2,64]{1,0:T(2,128)} %param.13) | copy-start | bytes 1540
  11.2 6.3 %copy-start.11 = (s32[2]{0:T(128)S(1)}, s32[2]{0:T(128)}, u32[]{:S(2)}) copy-start(s32[2]{0:T(128)} %param.14) | copy-start | bytes 28
  11.2 6.4 %copy-start.10 = (s32[2,16]{1,0:T(2,128)S(1)}, s32[2,16]{1,0:T(2,128)}, u32[]{:S(2)}) copy-start(s32[2,16]{1,0:T(2,128)} %param.17) | copy-start | bytes 388
  18.0 116.2 %copy-start.8 = (f32[2,16,2,64]{3,1,2,0:T(8,128)}, f32[2,16,2,64]{3,1,2,0:T(8,128)S(1)}, u32[]{:S(2)}) copy-start(f32[2,16,2,64]{3,1,2,0:T(8,128)S(1)} %get-tuple-element.124) | copy-start | bytes 49156
  18.0 116.2 %copy-start.9 = (f32[2,16,2,64]{3,1,2,0:T(8,128)}, f32[2,16,2,64]{3,1,2,0:T(8,128)S(1)}, u32[]{:S(2)}) copy-start(f32[2,16,2,64]{3,1,2,0:T(8,128)S(1)} %get-tuple-element.125) | copy-start | bytes 49156
  132.1 0.8 copy-start.6
  133.9 0.8 copy-start.1
  133.9 1.0 copy-start.3
  162.2 39.3 %copy-start.2 = (bf16[2,16,2,20,64]{4,3,1,2,0:T(8,128)(2,1)S(1)}, bf16[2,16,2,20,64]{4,3,1,2,0:T(8,128)(2,1)}, u32[]{:S(2)}) copy-start(bf16[2,16,2,20,64]{4,3,1,2,0:T(8,128)(2,1)} %copy-done.1) | copy-start | bytes 491524
  162.2 39.3 %copy-start.4 = (bf16[2,16,2,20,64]{4,3,1,2,0:T(8,128)(2,1)S(1)}, bf16[2,16,2,20,64]{4,3,1,2,0:T(8,128)(2,1)}, u32[]{:S(2)}) copy-start(bf16[2,16,2,20,64]{4,3,1,2,0:T(8,128)(2,1)} %copy-done.3) | copy-start | bytes 491524
  228.7 3.6 %copy-start.7 = (f32[8,2,16,2,4,5]{2,4,5,3,1,0:T(4,128)}, f32[8,2,16,2,4,5]{2,4,5,3,1,0:T(4,128)S(1)}, u32[]{:S(2)}) copy-start(f32[8,2,16,2,4,5]{2,4,5,3,1,0:T(4,128)S(1)} %all_gather.13) | copy-start | bytes 122884
  234.7 5.0 %slice-start = ((f32[8,2,16,2,4,5]{2,4,5,3,1,0:T(4,128)}), f32[7,2,16,2,4,5]{2,4,5,3,1,0:T(4,128)S(1)}, s32[]{:S(2)}) async-start(f32[8,2,16,2,4,5]{2,4,5,3,1,0:T(4,128)} %copy-done.7), calls=%async_computation.3 | async-start | bytes 573440 | tf_op jit(solution)/shard_map/slice | solution.py:18
Sparse Core Ops, SparseCore 0:
  11.3 92.0 reduce-scatter.1
  155.6 68.7 all-gather.3
where the time goes:
time: 268 us; the launch traced here: 267 us
  waiting for transfers between devices  85.4 us (32%)
  blocking collectives  78.7 us (29%)
  local copies, waits for them, and re-layouts  45.2 us (17%)
  matrix products  27.5 us (10%)
  other arithmetic  15.7 us (6%)
  between operations  13.8 us (5%)
    reduce_scatter x1, waiting for transfers between devices, local(): lax.psum_scatter(project_rows(hidden, w_qkv), 'row', scatter_dimension=0,...  85.4 us
    all_gather x2, blocking collectives, merged(): pieces = jax.tree.map(lambda part: lax.all_gather(part, axis), value)  51.9 us
    all_gather x1, blocking collectives, local(): projected = lax.all_gather(column_sums, 'col', axis=1, tiled=True)  26.7 us
    dynamic_slice x7, local copies, waits for them, and re-layouts, merged(): lax.scan(lambda total, section: (join(total, section), None), head, tail)  7.99 us
    dot_general x1, matrix products, local(): jnp.einsum('sr,sqkgd->rqkgd', owner_float, slot_acc, precision=lax.Precis...  7.38 us
    reduce_sum x1, other arithmetic, local(): slot_sums = jnp.sum(page_weights, axis=-1)  5.86 us
    dot_general x1, matrix products, local(): jnp.einsum('sqkgd,spkd->sqkgp', slot_queries, pool_keys.reshape(pool_slot...  5.66 us
    add x7, other arithmetic, combine_states(): acc_early * scale_early[..., None] + acc_late * scale_late[..., None]  5.49 us
  transfers between devices with their start and end apart: 2, of which 1 were waited for; matrix products, arithmetic and copies ran while one was open for 12% of the time, Pallas kernels for 0%

commit v1 on v0

--- a/solution.py
+++ b/solution.py
@@ -70,7 +70,12 @@
     column_sums = lax.psum_scatter(
         project_rows(hidden, w_qkv), "row", scatter_dimension=0, tiled=True
     ).astype(jnp.bfloat16)
-    projected = lax.all_gather(column_sums, "col", axis=1, tiled=True)
+    ring = [column_sums]
+    for hop in range(7):
+        ring.append(lax.ppermute(ring[-1], "col", [(dev, (dev + 1) % 8) for dev in range(8)]))
+    projected = jnp.roll(
+        jnp.concatenate(ring[::-1], axis=1), (lax.axis_index("col") + 1) * ring[0].shape[1], axis=1
+    )
     prompts_here = prompt_lengths.shape[0]
     projected = projected.reshape(prompts_here, SAMPLES, 2, projected.shape[-1])
     steps_ahead = jnp.arange(2, dtype=jnp.int32)

time: 268 us -> 282 us (1.052)
  waiting for transfers between devices: 85.4 us -> 123 us
  blocking collectives: 78.7 us -> 52.7 us
    ppermute x0 -> x7, waiting for transfers between devices: none -> 30.9 us  [local(): lax.ppermute(ring[-1], 'col', [(dev, (dev + 1) % 8) for dev in range(8)])]
    all_gather x1 -> x0, blocking collectives: 26.7 us -> none  [local(): projected = lax.all_gather(column_sums, 'col', axis=1, tiled=True)]
    reduce_scatter x1, waiting for transfers between devices: 85.4 us -> 91.7 us  [local(): lax.psum_scatter(project_rows(hidden, w_qkv), 'row', scatter_dimension=0,...]
  transfers between devices with their start and end apart: 2 -> 9, of which waited for: 1 -> 7; matrix products, arithmetic and copies ran while one was open for 12% -> 12% of each run, Pallas kernels for 0% -> 0%
where the time goes in v1:
time: 282 us; the launch traced here: 280 us
  waiting for transfers between devices  123 us (44%)
  blocking collectives  52.7 us (19%)
  local copies, waits for them, and re-layouts  44.9 us (16%)
  matrix products  27.4 us (10%)
  other arithmetic  15.8 us (6%)
  between operations  13.8 us (5%)
    reduce_scatter x1, waiting for transfers between devices, local(): lax.psum_scatter(project_rows(hidden, w_qkv), 'row', scatter_dimension=0,...  91.7 us
    all_gather x2, blocking collectives, merged(): pieces = jax.tree.map(lambda part: lax.all_gather(part, axis), value)  52.7 us
    ppermute x7, waiting for transfers between devices, local(): lax.ppermute(ring[-1], 'col', [(dev, (dev + 1) % 8) for dev in range(8)])  30.9 us
    dynamic_slice x7, local copies, waits for them, and re-layouts, merged(): lax.scan(lambda total, section: (join(total, section), None), head, tail)  7.99 us
    dot_general x1, matrix products, local(): jnp.einsum('sr,sqkgd->rqkgd', owner_float, slot_acc, precision=lax.Precis...  7.38 us
    reduce_sum x1, other arithmetic, local(): slot_sums = jnp.sum(page_weights, axis=-1)  5.95 us
  transfers between devices with their start and end apart: 9, of which 7 were waited for; matrix products, arithmetic and copies ran while one was open for 12% of the time, Pallas kernels for 0%

profile of v1, /device:TPU:6, one launch (start us, length us, event | category | flops | bytes accessed | tf_op | source)
XLA Modules:
  0.0 280.3 jit_solution(1527132033127091374)
XLA Ops:
  6.6 0.9 copy-done
  7.5 3.6 %fusion.110 = f32[2048,448]{1,0:T(8,128)} fusion(bf16[2048,80]{0,1:T(8,128)(2,1)S(1)} %copy-done, bf16[80,448]{1,0:T(8,128)(2,1)} %param.12), kind=kOutput, calls=%fused_computation.142 | convolution fusion | flops 146800640 | bytes 4069376 | tf_op jit(solution)/shard_map/dot_general | solution.py:52
  11.7 91.7 %reduce-scatter.2.cloned.1.call-done = f32[64,448]{1,0:T(8,128)} async-done(((f32[2048,448]{1,0:T(8,128)}), f32[64,448]{1,0:T(8,128)}) %reduce-scatter.2.cloned.1.call-update) | async-done | bytes 114704 | tf_op jit(solution)/shard_map/reduce_scatter | solution.py:70
  103.5 0.9 convert_element_type.48
  104.4 1.6 collective-permute-start
  106.0 4.0 %collective-permute-done = bf16[64,448]{1,0:T(8,128)(2,1)S(1)} collective-permute-done((bf16[64,448]{1,0:T(8,128)(2,1)S(1)}, bf16[64,448]{1,0:T(8,128)(2,1)S(1)}, u32[]{:S(2)}, u32[]{:S(2)}) %collective-permute-start) | collective-permute-done | bytes 57376 | tf_op jit(solution)/shard_map/ppermute | solution.py:75
  110.0 1.0 collective-permute-start.1
  111.0 5.1 %collective-permute-done.1 = bf16[64,448]{1,0:T(8,128)(2,1)S(1)} collective-permute-done((bf16[64,448]{1,0:T(8,128)(2,1)S(1)}, bf16[64,448]{1,0:T(8,128)(2,1)S(1)}, u32[]{:S(2)}, u32[]{:S(2)}) %collective-permute-start.1) | collective-permute-done | bytes 57376 | tf_op jit(solution)/shard_map/ppermute | solution.py:75
  116.2 5.4 %collective-permute-done.2 = bf16[64,448]{1,0:T(8,128)(2,1)S(1)} collective-permute-done((bf16[64,448]{1,0:T(8,128)(2,1)S(1)}, bf16[64,448]{1,0:T(8,128)(2,1)S(1)}, u32[]{:S(2)}, u32[]{:S(2)}) %collective-permute-start.2) | collective-permute-done | bytes 57376 | tf_op jit(solution)/shard_map/ppermute | solution.py:75
  121.6 5.5 %collective-permute-done.3 = bf16[64,448]{1,0:T(8,128)(2,1)S(1)} collective-permute-done((bf16[64,448]{1,0:T(8,128)(2,1)S(1)}, bf16[64,448]{1,0:T(8,128)(2,1)S(1)}, u32[]{:S(2)}, u32[]{:S(2)}) %collective-permute-start.3) | collective-permute-done | bytes 57376 | tf_op jit(solution)/shard_map/ppermute | solution.py:75
  127.1 5.5 %collective-permute-done.4 = bf16[64,448]{1,0:T(8,128)(2,1)S(1)} collective-permute-done((bf16[64,448]{1,0:T(8,128)(2,1)S(1)}, bf16[64,448]{1,0:T(8,128)(2,1)S(1)}, u32[]{:S(2)}, u32[]{:S(2)}) %collective-permute-start.4) | collective-permute-done | bytes 57376 | tf_op jit(solution)/shard_map/ppermute | solution.py:75
  132.6 2.1 reshape_squeeze.6
  134.7 4.0 %reshape_squeeze.7 = bf16[16,128,4,128]{3,2,1,0:T(4,128)(2,1)} reshape(bf16[1,16,128,512]{3,2,1,0:T(8,128)(2,1)} %param.16) | data formatting | bytes 4194304 | tf_op jit(solution)/shard_map/reshape;squeeze | solution.py:131
  138.7 5.5 %collective-permute-done.6 = bf16[64,448]{1,0:T(8,128)(2,1)S(1)} collective-permute-done((bf16[64,448]{1,0:T(8,128)(2,1)S(1)}, bf16[64,448]{1,0:T(8,128)(2,1)S(1)}, u32[]{:S(2)}, u32[]{:S(2)}) %collective-permute-start.6) | collective-permute-done | bytes 57376 | tf_op jit(solution)/shard_map/ppermute | solution.py:75
  144.1 0.5 concatenate.22
  145.1 0.8 copy-done.6
  145.8 0.2 slice.58
  146.1 0.2 reshape.182
  146.5 0.3 fusion.63
  146.8 0.3 copy.163
  147.1 0.3 copy.162
  147.8 1.1 gather_fusion
  148.9 5.6 %bitcast_reduce_fusion = (f32[16,32,4,5]{1,3,2,0:T(8,128)S(1)}, f32[16,4,32,5,128]{4,2,3,1,0:T(8,128)}) fusion(pred[16,128]{1,0:T(8,128)(4,1)S(1)} %add_compare_fusion, bf16[16,128,4,128,1]{3,2,1,0,4:T(4,128)(2,1)} %bitcast.107, bf16[16,32,4,5,128]{4,1,3,2,0:T(8,128)(2,1)S(1)} %gather_fusion, pred[16]{0:T(512)(128)(4,1)S(1)} %compare_and_fusion), kind=kOutput, calls=%fused_computation.13 | convolution fusion | flops 340776960 | bytes 10004496 | tf_op jit(solution)/shard_map/sqkgd,spkd->sqkgp/dot_general | solution.py:112
  154.7 0.6 gather_fusion.1
  155.5 4.2 %fusion.21 = f32[16,32,4,5,128]{4,1,3,2,0:T(8,128)S(1)} fusion(f32[16,4,32,5,128]{4,2,3,1,0:T(8,128)} %get-tuple-element.131, f32[16,32,4,5]{1,3,2,0:T(8,128)S(1)} %copy.169, pred[16,128]{1,0:T(8,128)(4,1)S(1)} %add_compare_fusion, bf16[16,128,4,128,1]{3,2,1,0,4:T(4,128)(2,1)} %bitcast.106), kind=kOutput, calls=%fused_computation.31 | convolution fusion | flops 342097920 | bytes 12625920 | tf_op jit(solution)/shard_map/sqkgp,spkd->sqkgd/dot_general | solution.py:128
  159.8 7.4 %fusion.6 = f32[2,32,4,5,128]{4,0,3,2,1:T(2,128)S(1)} fusion(f32[16,32,4,5,128]{4,1,3,2,0:T(8,128)S(1)} %fusion.21, s32[16,2]{0,1:T(2,128)S(1)} %get-tuple-element.90), kind=kOutput, calls=%fused_computation.16 | convolution fusion | flops 31457312 | bytes 5898368 | tf_op jit(solution)/shard_map/sr,sqkgd->rqkgd/dot_general | solution.py:138
  167.2 1.1 copy.175
  168.3 2.6 reshape.151
  170.8 4.0 %reshape.153 = bf16[2,2,512,4,128]{4,3,2,1,0:T(4,128)(2,1)} reshape(bf16[2,2,512,512]{3,2,1,0:T(8,128)(2,1)} %param.19) | data formatting | bytes 4194304 | tf_op jit(solution)/shard_map/reshape | solution.py:186
  175.0 0.8 copy.166
  175.8 6.0 %fusion.9 = f32[16,32,4,5]{1,3,2,0:T(8,128)} fusion(f32[16,4,32,5,128]{4,2,3,1,0:T(8,128)} %get-tuple-element.131, f32[16,32,4,5]{1,3,2,0:T(8,128)S(1)} %copy.169, pred[16,128]{1,0:T(8,128)(4,1)S(1)} %add_compare_fusion), kind=kLoop, calls=%fused_computation.20 | loop fusion | flops 6543360 | bytes 5326848 | tf_op jit(solution)/shard_map/reduce_sum | solution.py:127
  181.8 1.1 copy.170
  182.9 2.4 fusion.66
  185.3 26.7 %all-gather = f32[16,16,2,4,5]{1,3,4,2,0:T(4,128)S(1)} all-gather(f32[2,16,2,4,5]{1,3,4,2,0:T(4,128)S(1)} %copy.172), channel_id=2, replica_groups=mesh['row'=32,'col'=8] {'col'}, dimensions={0}, use_global_device_ids=true | all-gather | bytes 46080 | tf_op jit(solution)/shard_map/all_gather | solution.py:16
  212.0 1.6 fusion.105
  213.7 1.5 reshape.183
  215.3 1.1 copy.167
  216.4 26.0 %all_gather.9 = f32[8,2,16,2,4,5]{2,4,5,3,1,0:T(4,128)S(1)} all-gather(f32[1,2,16,2,4,5]{2,4,5,3,1,0:T(4,128)S(1)} %copy.167), channel_id=1, replica_groups=mesh['row'=32,'col'=8] {'col'}, dimensions={0}, use_global_device_ids=true | all-gather | bytes 46080 | tf_op jit(solution)/shard_map/all_gather | solution.py:16
  242.4 1.1 fusion.107
  243.5 0.8 fusion.73
  244.4 0.4 fusion.109
  244.8 0.8 fusion.108
  245.7 0.3 fusion.64
  246.0 1.0 convolution_bitcast_fusion
  247.0 1.1 slice_bitcast_fusion
  248.2 0.2 copy.176
  248.4 5.0 %slice.66 = f32[7,2,16,2,4,5,128]{6,2,5,4,3,1,0:T(8,128)} slice(f32[8,2,16,2,4,5,128]{6,2,5,4,3,1,0:T(8,128)} %all-gather.3.cloned.1.call-done), slice={[1:8], [0:2], [0:16], [0:2], [0:4], [0:5], [0:128]} | slice | bytes 9175040 | tf_op jit(solution)/shard_map/slice | solution.py:18
  253.5 16.7 %while.14 = (s32[]{:T(128)}, f32[2,16,2,4,5]{1,3,4,2,0:T(4,128)S(1)}, f32[2,16,2,4,5]{1,3,4,2,0:T(4,128)S(1)}, f32[2,16,2,4,5,128]{5,4,3,2,1,0:T(8,128)S(1)}, f3...) while((s32[]{:T(128)}, ...), condition=%wide.region_9.10_spmd, body=%wide.region_8.9_spmd.sunk | while | flops 499202 | bytes 3348581 | solution.py:19
  253.9 1.1 constant_dynamic-slice_fusion.4
  255.0 0.8 fusion.117
  256.3 1.1 constant_dynamic-slice_fusion.4
  257.4 0.8 fusion.117
  258.7 1.1 constant_dynamic-slice_fusion.4
  259.8 0.8 fusion.117
  261.1 1.1 constant_dynamic-slice_fusion.4
  262.2 0.8 fusion.117
  263.4 1.1 constant_dynamic-slice_fusion.4
  264.6 0.8 fusion.117
  265.8 1.1 constant_dynamic-slice_fusion.4
  267.0 0.8 fusion.117
  268.2 1.1 constant_dynamic-slice_fusion.4
  269.4 0.8 fusion.117
  270.6 2.1 fusion.55
  272.8 0.7 convert_element_type.59
  (96 shorter events, 6.2 us)
Async XLA Ops:
  6.5 1.0 copy-start
  6.5 4.6 %copy-start.12 = (s32[2,64]{1,0:T(2,128)S(1)}, s32[2,64]{1,0:T(2,128)}, u32[]{:S(2)}) copy-start(s32[2,64]{1,0:T(2,128)} %param.13) | copy-start | bytes 1540
  6.5 4.9 %copy-start.10 = (s32[2,16]{1,0:T(2,128)S(1)}, s32[2,16]{1,0:T(2,128)}, u32[]{:S(2)}) copy-start(s32[2,16]{1,0:T(2,128)} %param.17) | copy-start | bytes 388
  6.5 4.9 %copy-start.11 = (s32[2]{0:T(128)S(1)}, s32[2]{0:T(128)}, u32[]{:S(2)}) copy-start(s32[2]{0:T(128)} %param.14) | copy-start | bytes 28
  6.5 126.1 %copy-start.5 = (bf16[1,16,128,512]{3,2,1,0:T(8,128)(2,1)S(1)}, bf16[1,16,128,512]{3,2,1,0:T(8,128)(2,1)}, u32[]{:S(2)}) copy-start(bf16[1,16,128,512]{3,2,1,0:T(8,128)(2,1)} %param.15) | copy-start | bytes 6291460
  6.5 96.9 %reduce-scatter.2.cloned.1.call-start = ((), (), s32[]{:S(2)}) async-start(), calls=%async_computation.1 | async-start | bytes 4325376 | tf_op jit(solution)/shard_map/reduce_scatter | solution.py:70
  11.1 235.9 %all-gather.3.cloned.1.call-start = ((), (), s32[]{:S(2)}) async-start(), calls=%async_computation.2 | async-start | bytes 5898240 | tf_op jit(solution)/shard_map/all_gather | solution.py:16
  11.7 134.8 %copy-start.8 = (f32[2,16,2,64]{3,1,2,0:T(8,128)}, f32[2,16,2,64]{3,1,2,0:T(8,128)S(1)}, u32[]{:S(2)}) copy-start(f32[2,16,2,64]{3,1,2,0:T(8,128)S(1)} %get-tuple-element.124) | copy-start | bytes 49156
  11.7 134.8 %copy-start.9 = (f32[2,16,2,64]{3,1,2,0:T(8,128)}, f32[2,16,2,64]{3,1,2,0:T(8,128)S(1)}, u32[]{:S(2)}) copy-start(f32[2,16,2,64]{3,1,2,0:T(8,128)S(1)} %get-tuple-element.125) | copy-start | bytes 49156
  104.4 5.6 %collective-permute-start = (bf16[64,448]{1,0:T(8,128)(2,1)S(1)}, bf16[64,448]{1,0:T(8,128)(2,1)S(1)}, u32[]{:S(2)}, u32[]{:S(2)}) collective-permute-start(bf16[64,448]{1,0:T(8,128)(2,1)S(1)} %convert_element_type.48), channel_id=1, source_target_pairs={{0,1},{1,2},{2,3},{3,4},{4,5},{5,6},{6,7},{7,0},{8,9},{9,10},{10,1... | collective-permute-start | bytes 172040 | tf_op jit(solution)/shard_map/ppermute | solution.py:75
  110.0 6.1 %collective-permute-start.1 = (bf16[64,448]{1,0:T(8,128)(2,1)S(1)}, bf16[64,448]{1,0:T(8,128)(2,1)S(1)}, u32[]{:S(2)}, u32[]{:S(2)}) collective-permute-start(bf16[64,448]{1,0:T(8,128)(2,1)S(1)} %collective-permute-done), channel_id=1, source_target_pairs={{0,1},{1,2},{2,3},{3,4},{4,5},{5,6},{6,7},{7,0},{8,9},{9,10},{10,1... | collective-permute-start | bytes 172040 | tf_op jit(solution)/shard_map/ppermute | solution.py:75
  116.2 5.5 %collective-permute-start.2 = (bf16[64,448]{1,0:T(8,128)(2,1)S(1)}, bf16[64,448]{1,0:T(8,128)(2,1)S(1)}, u32[]{:S(2)}, u32[]{:S(2)}) collective-permute-start(bf16[64,448]{1,0:T(8,128)(2,1)S(1)} %collective-permute-done.1), channel_id=1, source_target_pairs={{0,1},{1,2},{2,3},{3,4},{4,5},{5,6},{6,7},{7,0},{8,9},{9,10},{10,1... | collective-permute-start | bytes 172040 | tf_op jit(solution)/shard_map/ppermute | solution.py:75
  121.6 5.5 %collective-permute-start.3 = (bf16[64,448]{1,0:T(8,128)(2,1)S(1)}, bf16[64,448]{1,0:T(8,128)(2,1)S(1)}, u32[]{:S(2)}, u32[]{:S(2)}) collective-permute-start(bf16[64,448]{1,0:T(8,128)(2,1)S(1)} %collective-permute-done.2), channel_id=1, source_target_pairs={{0,1},{1,2},{2,3},{3,4},{4,5},{5,6},{6,7},{7,0},{8,9},{9,10},{10,1... | collective-permute-start | bytes 172040 | tf_op jit(solution)/shard_map/ppermute | solution.py:75
  127.1 5.5 %collective-permute-start.4 = (bf16[64,448]{1,0:T(8,128)(2,1)S(1)}, bf16[64,448]{1,0:T(8,128)(2,1)S(1)}, u32[]{:S(2)}, u32[]{:S(2)}) collective-permute-start(bf16[64,448]{1,0:T(8,128)(2,1)S(1)} %collective-permute-done.3), channel_id=1, source_target_pairs={{0,1},{1,2},{2,3},{3,4},{4,5},{5,6},{6,7},{7,0},{8,9},{9,10},{10,1... | collective-permute-start | bytes 172040 | tf_op jit(solution)/shard_map/ppermute | solution.py:75
  132.6 6.1 %collective-permute-start.5 = (bf16[64,448]{1,0:T(8,128)(2,1)S(1)}, bf16[64,448]{1,0:T(8,128)(2,1)S(1)}, u32[]{:S(2)}, u32[]{:S(2)}) collective-permute-start(bf16[64,448]{1,0:T(8,128)(2,1)S(1)} %collective-permute-done.4), channel_id=1, source_target_pairs={{0,1},{1,2},{2,3},{3,4},{4,5},{5,6},{6,7},{7,0},{8,9},{9,10},{10,1... | collective-permute-start | bytes 172040 | tf_op jit(solution)/shard_map/ppermute | solution.py:75
  138.7 5.5 %collective-permute-start.6 = (bf16[64,448]{1,0:T(8,128)(2,1)S(1)}, bf16[64,448]{1,0:T(8,128)(2,1)S(1)}, u32[]{:S(2)}, u32[]{:S(2)}) collective-permute-start(bf16[64,448]{1,0:T(8,128)(2,1)S(1)} %collective-permute-done.5), channel_id=1, source_target_pairs={{0,1},{1,2},{2,3},{3,4},{4,5},{5,6},{6,7},{7,0},{8,9},{9,10},{10,1... | collective-permute-start | bytes 172040 | tf_op jit(solution)/shard_map/ppermute | solution.py:75
  145.1 0.8 copy-start.6
  146.8 0.7 copy-start.1
  146.8 0.9 copy-start.3
  175.0 40.2 %copy-start.2 = (bf16[2,16,2,20,64]{4,3,1,2,0:T(8,128)(2,1)S(1)}, bf16[2,16,2,20,64]{4,3,1,2,0:T(8,128)(2,1)}, u32[]{:S(2)}) copy-start(bf16[2,16,2,20,64]{4,3,1,2,0:T(8,128)(2,1)} %copy-done.1) | copy-start | bytes 491524
  175.0 40.2 %copy-start.4 = (bf16[2,16,2,20,64]{4,3,1,2,0:T(8,128)(2,1)S(1)}, bf16[2,16,2,20,64]{4,3,1,2,0:T(8,128)(2,1)}, u32[]{:S(2)}) copy-start(bf16[2,16,2,20,64]{4,3,1,2,0:T(8,128)(2,1)} %copy-done.3) | copy-start | bytes 491524
  242.4 3.6 %copy-start.7 = (f32[8,2,16,2,4,5]{2,4,5,3,1,0:T(4,128)}, f32[8,2,16,2,4,5]{2,4,5,3,1,0:T(4,128)S(1)}, u32[]{:S(2)}) copy-start(f32[8,2,16,2,4,5]{2,4,5,3,1,0:T(4,128)S(1)} %all_gather.9) | copy-start | bytes 122884
  248.4 5.0 %slice-start = ((f32[8,2,16,2,4,5]{2,4,5,3,1,0:T(4,128)}), f32[7,2,16,2,4,5]{2,4,5,3,1,0:T(4,128)S(1)}, s32[]{:S(2)}) async-start(f32[8,2,16,2,4,5]{2,4,5,3,1,0:T(4,128)} %copy-done.7), calls=%async_computation.3 | async-start | bytes 573440 | tf_op jit(solution)/shard_map/slice | solution.py:18
Sparse Core Ops, SparseCore 0:
  11.3 92.0 reduce-scatter.1
  168.4 69.5 all-gather.2
